TPU v7x, 128 devices: a whole 4x4x4 slice. The times are simulated.
128 devices in a mesh: tile: 8 (over x_hi, z), src: 16 (over y, x_lo, core).
Axes of the slice: x: 4 (x_hi: 2, x_lo: 2; x = x_hi * 2 + x_lo), y: 4, z: 4, core: 2. Of those that a mesh axis runs over, the one named last changes fastest.
Arguments:
- permittivity: float32 [128, 16, 320], P(('tile', 'src')), may hold values from 1 to 2
- e_start: float32 [16, 3, 128, 16, 320], P('src', None, 'tile'), may hold values from -6 to 6
- h_start: float32 [16, 3, 128, 16, 320], P('src', None, 'tile'), may hold values from -6 to 6
- e_cotangent: float32 [16, 3, 128, 16, 320], P('src', None, 'tile'), may hold values from -6 to 6
- h_cotangent: float32 [16, 3, 128, 16, 320], P('src', None, 'tile'), may hold values from -6 to 6
Outputs:
- e_final: float32 [16, 3, 128, 16, 320], P('src', None, 'tile')
- gradient: float32 [128, 16, 320], P(('tile', 'src'))
All inputs are finite; a program needn't handle non-finite values.
Results may differ from a plain program's by a relative error of at most 0.00002.
Values sent between devices are 32-bit elements; how exact they have to be, the bound alone decides.
No kernel may reach another device: no remote copies, remote signals or barrier semaphores. Data moves between devices by JAX's collectives and lax.ppermute only.
A program may use at most 64 MiB of HBM per device.

v0:
```python
import jax
import jax.numpy as jnp
from jax import lax
from jax.sharding import PartitionSpec as P

STEPS = 6
courant = 0.57


def passed_along(array, axis, by):
    length = lax.axis_size(axis)
    pairs = [(i, i + by) for i in range(length) if 0 <= i + by < length]
    return lax.ppermute(array, axis, pairs)


def ahead_local(field, axis):
    size = field.shape[axis]
    upper = lax.slice_in_dim(field, 1, size, axis=axis)
    zeros = jnp.zeros_like(lax.slice_in_dim(field, 0, 1, axis=axis))
    return jnp.concatenate([upper, zeros], axis) - field


def behind_local(field, axis):
    size = field.shape[axis]
    lower = lax.slice_in_dim(field, 0, size - 1, axis=axis)
    zeros = jnp.zeros_like(lax.slice_in_dim(field, 0, 1, axis=axis))
    return field - jnp.concatenate([zeros, lower], axis)


def curl_ahead(field):
    border = passed_along(field[1:3, 0:1], "tile", -1)
    ahead_one = jnp.concatenate([field[1, 1:], border[0]], 0) - field[1]
    ahead_two = jnp.concatenate([field[2, 1:], border[1]], 0) - field[2]
    return jnp.stack(
        [
            ahead_local(field[2], 1) - ahead_local(field[1], 2),
            ahead_local(field[0], 2) - ahead_two,
            ahead_one - ahead_local(field[0], 1),
        ]
    )


def curl_behind(field):
    border = passed_along(field[1:3, -1:], "tile", 1)
    behind_one = field[1] - jnp.concatenate([border[0], field[1, :-1]], 0)
    behind_two = field[2] - jnp.concatenate([border[1], field[2, :-1]], 0)
    return jnp.stack(
        [
            behind_local(field[2], 1) - behind_local(field[1], 2),
            behind_local(field[0], 2) - behind_two,
            behind_one - behind_local(field[0], 1),
        ]
    )


def add_term(term, shard_total, local_total):
    shard_total = shard_total + lax.psum_scatter(term, "src", scatter_dimension=0, tiled=True)
    return (shard_total, local_total)


def on_device(permittivity, e_start, h_start, e_cotangent, h_cotangent):
    window = lax.all_gather(permittivity, "src", axis=0, tiled=True)
    inverse = 1.0 / window
    efield = e_start[0]
    hfield = h_start[0]
    stored = []
    for turn in range(STEPS):
        hfield = hfield - courant * curl_ahead(efield)
        curled = curl_behind(hfield)
        efield = efield + courant * inverse * curled
        stored.append(curled)
    adj_efield = e_cotangent[0]
    adj_hfield = h_cotangent[0]
    shard_total = jnp.zeros(permittivity.shape, jnp.float32)
    local_total = jnp.zeros(window.shape, jnp.float32)
    for turn in range(STEPS - 1, -1, -1):
        curled = stored[turn]
        term = courant * jnp.sum(adj_efield * curled, axis=0)
        shard_total, local_total = add_term(term, shard_total, local_total)
        adj_hfield = adj_hfield + courant * curl_ahead(inverse * adj_efield)
        adj_efield = adj_efield - courant * curl_behind(adj_hfield)
    gradient = -shard_total / (permittivity * permittivity)
    return (efield[None], gradient)


def solution(mesh):
    in_specs = (
        P(("tile", "src"), None, None),
        P("src", None, "tile", None, None),
        P("src", None, "tile", None, None),
        P("src", None, "tile", None, None),
        P("src", None, "tile", None, None),
    )
    out_specs = (P("src", None, "tile", None, None), P(("tile", "src"), None, None))
    return jax.shard_map(
        on_device, mesh=mesh, in_specs=in_specs, out_specs=out_specs, check_vma=False
    )
```

profile of v0, /device:TPU:0, one launch (start us, length us, event | category | flops | bytes accessed | tf_op | source)
XLA Modules:
  0.0 292.2 jit_solution(3197136223210983773)
XLA Ops:
  8.0 1.4 collective-permute-start
  9.4 1.3 slice_bitcast_fusion.65
  10.8 21.7 %all_gather.3 = f32[16,16,320]{2,1,0:T(8,128)S(1)} all-gather(f32[1,16,320]{2,1,0:T(8,128)S(1)} %copy-done.17), channel_id=1, replica_groups=mesh['tile'=8,'src'=16] {'src'}, dimensions={0}, use_global_device_ids=true | all-gather | bytes 348160 | tf_op jit(solution)/shard_map/all_gather | solution.py:62
  34.6 4.5 %collective-permute-start.1 = (f32[2,1,16,320]{3,2,1,0:T(8,128)S(1)}, f32[2,1,16,320]{3,2,1,0:T(8,128)S(1)}, u32[]{:S(2)}, u32[]{:S(2)}) collective-permute-start(f32[2,1,16,320]{3,2,1,0:T(8,128)S(1)} %slice.1140), channel_id=1, source_target_pairs={{0,16},{16,32},{32,48},{48,64},{64,80},{80,96},{96,112},{1,17},{17... | collective-permute-start | bytes 122888 | tf_op jit(solution)/shard_map/ppermute | solution.py:13
  39.2 1.7 collective-permute-done.1
  41.7 1.3 collective-permute-start.2
  43.4 4.5 %collective-permute-done.2 = f32[2,1,16,320]{3,2,1,0:T(8,128)S(1)} collective-permute-done((f32[2,1,16,320]{3,2,1,0:T(8,128)S(1)}, f32[2,1,16,320]{3,2,1,0:T(8,128)S(1)}, u32[]{:S(2)}, u32[]{:S(2)}) %collective-permute-start.2) | collective-permute-done | bytes 40992 | tf_op jit(solution)/shard_map/ppermute | solution.py:13
  48.6 3.9 %collective-permute-start.3 = (f32[2,1,16,320]{3,2,1,0:T(8,128)S(1)}, f32[2,1,16,320]{3,2,1,0:T(8,128)S(1)}, u32[]{:S(2)}, u32[]{:S(2)}) collective-permute-start(f32[2,1,16,320]{3,2,1,0:T(8,128)S(1)} %slice.1164), channel_id=1, source_target_pairs={{0,16},{16,32},{32,48},{48,64},{64,80},{80,96},{96,112},{1,17},{17... | collective-permute-start | bytes 122888 | tf_op jit(solution)/shard_map/ppermute | solution.py:13
  52.6 1.7 collective-permute-done.3
  55.1 1.3 collective-permute-start.4
  56.9 7.5 %collective-permute-done.4 = f32[2,1,16,320]{3,2,1,0:T(8,128)S(1)} collective-permute-done((f32[2,1,16,320]{3,2,1,0:T(8,128)S(1)}, f32[2,1,16,320]{3,2,1,0:T(8,128)S(1)}, u32[]{:S(2)}, u32[]{:S(2)}) %collective-permute-start.4) | collective-permute-done | bytes 40992 | tf_op jit(solution)/shard_map/ppermute | solution.py:13
  65.2 7.9 %collective-permute-start.5 = (f32[2,1,16,320]{3,2,1,0:T(8,128)S(1)}, f32[2,1,16,320]{3,2,1,0:T(8,128)S(1)}, u32[]{:S(2)}, u32[]{:S(2)}) collective-permute-start(f32[2,1,16,320]{3,2,1,0:T(8,128)S(1)} %slice.1188), channel_id=1, source_target_pairs={{0,16},{16,32},{32,48},{48,64},{64,80},{80,96},{96,112},{1,17},{17... | collective-permute-start | bytes 122888 | tf_op jit(solution)/shard_map/ppermute | solution.py:13
  73.1 1.7 collective-permute-done.5
  75.8 1.3 collective-permute-start.6
  77.5 4.5 %collective-permute-done.6 = f32[2,1,16,320]{3,2,1,0:T(8,128)S(1)} collective-permute-done((f32[2,1,16,320]{3,2,1,0:T(8,128)S(1)}, f32[2,1,16,320]{3,2,1,0:T(8,128)S(1)}, u32[]{:S(2)}, u32[]{:S(2)}) %collective-permute-start.6) | collective-permute-done | bytes 40992 | tf_op jit(solution)/shard_map/ppermute | solution.py:13
  82.9 7.5 %collective-permute-start.7 = (f32[2,1,16,320]{3,2,1,0:T(8,128)S(1)}, f32[2,1,16,320]{3,2,1,0:T(8,128)S(1)}, u32[]{:S(2)}, u32[]{:S(2)}) collective-permute-start(f32[2,1,16,320]{3,2,1,0:T(8,128)S(1)} %slice.1212), channel_id=1, source_target_pairs={{0,16},{16,32},{32,48},{48,64},{64,80},{80,96},{96,112},{1,17},{17... | collective-permute-start | bytes 122888 | tf_op jit(solution)/shard_map/ppermute | solution.py:13
  90.5 1.7 collective-permute-done.7
  93.2 1.3 collective-permute-start.8
  95.0 4.5 %collective-permute-done.8 = f32[2,1,16,320]{3,2,1,0:T(8,128)S(1)} collective-permute-done((f32[2,1,16,320]{3,2,1,0:T(8,128)S(1)}, f32[2,1,16,320]{3,2,1,0:T(8,128)S(1)}, u32[]{:S(2)}, u32[]{:S(2)}) %collective-permute-start.8) | collective-permute-done | bytes 40992 | tf_op jit(solution)/shard_map/ppermute | solution.py:13
  100.4 7.5 %collective-permute-start.9 = (f32[2,1,16,320]{3,2,1,0:T(8,128)S(1)}, f32[2,1,16,320]{3,2,1,0:T(8,128)S(1)}, u32[]{:S(2)}, u32[]{:S(2)}) collective-permute-start(f32[2,1,16,320]{3,2,1,0:T(8,128)S(1)} %slice.1236), channel_id=1, source_target_pairs={{0,16},{16,32},{32,48},{48,64},{64,80},{80,96},{96,112},{1,17},{17... | collective-permute-start | bytes 122888 | tf_op jit(solution)/shard_map/ppermute | solution.py:13
  108.0 1.7 collective-permute-done.9
  110.8 1.5 collective-permute-start.10
  112.8 4.4 %collective-permute-done.10 = f32[2,1,16,320]{3,2,1,0:T(8,128)S(1)} collective-permute-done((f32[2,1,16,320]{3,2,1,0:T(8,128)S(1)}, f32[2,1,16,320]{3,2,1,0:T(8,128)S(1)}, u32[]{:S(2)}, u32[]{:S(2)}) %collective-permute-start.10) | collective-permute-done | bytes 40992 | tf_op jit(solution)/shard_map/ppermute | solution.py:13
  118.2 7.5 %collective-permute-start.11 = (f32[2,1,16,320]{3,2,1,0:T(8,128)S(1)}, f32[2,1,16,320]{3,2,1,0:T(8,128)S(1)}, u32[]{:S(2)}, u32[]{:S(2)}) collective-permute-start(f32[2,1,16,320]{3,2,1,0:T(8,128)S(1)} %slice.1260), channel_id=1, source_target_pairs={{0,16},{16,32},{32,48},{48,64},{64,80},{80,96},{96,112},{1,17},{17... | collective-permute-start | bytes 122888 | tf_op jit(solution)/shard_map/ppermute | solution.py:13
  125.8 1.7 collective-permute-done.11
  129.1 1.3 collective-permute-start.12
  130.9 4.5 %collective-permute-done.12 = f32[2,1,16,320]{3,2,1,0:T(8,128)S(1)} collective-permute-done((f32[2,1,16,320]{3,2,1,0:T(8,128)S(1)}, f32[2,1,16,320]{3,2,1,0:T(8,128)S(1)}, u32[]{:S(2)}, u32[]{:S(2)}) %collective-permute-start.12) | collective-permute-done | bytes 40992 | tf_op jit(solution)/shard_map/ppermute | solution.py:13
  137.0 7.5 %collective-permute-start.13 = (f32[2,1,16,320]{3,2,1,0:T(8,128)S(1)}, f32[2,1,16,320]{3,2,1,0:T(8,128)S(1)}, u32[]{:S(2)}, u32[]{:S(2)}) collective-permute-start(f32[2,1,16,320]{3,2,1,0:T(8,128)S(1)} %slice.1284), channel_id=1, source_target_pairs={{0,16},{16,32},{32,48},{48,64},{64,80},{80,96},{96,112},{1,17},{17... | collective-permute-start | bytes 122888 | tf_op jit(solution)/shard_map/ppermute | solution.py:13
  144.6 1.7 collective-permute-done.13
  147.1 1.3 collective-permute-start.14
  148.9 4.5 %collective-permute-done.14 = f32[2,1,16,320]{3,2,1,0:T(8,128)S(1)} collective-permute-done((f32[2,1,16,320]{3,2,1,0:T(8,128)S(1)}, f32[2,1,16,320]{3,2,1,0:T(8,128)S(1)}, u32[]{:S(2)}, u32[]{:S(2)}) %collective-permute-start.14) | collective-permute-done | bytes 40992 | tf_op jit(solution)/shard_map/ppermute | solution.py:13
  154.1 7.5 %collective-permute-start.15 = (f32[2,1,16,320]{3,2,1,0:T(8,128)S(1)}, f32[2,1,16,320]{3,2,1,0:T(8,128)S(1)}, u32[]{:S(2)}, u32[]{:S(2)}) collective-permute-start(f32[2,1,16,320]{3,2,1,0:T(8,128)S(1)} %slice.1308), channel_id=1, source_target_pairs={{0,16},{16,32},{32,48},{48,64},{64,80},{80,96},{96,112},{1,17},{17... | collective-permute-start | bytes 122888 | tf_op jit(solution)/shard_map/ppermute | solution.py:13
  161.7 1.7 collective-permute-done.15
  164.5 1.3 collective-permute-start.16
  166.3 4.7 %collective-permute-done.16 = f32[2,1,16,320]{3,2,1,0:T(8,128)S(1)} collective-permute-done((f32[2,1,16,320]{3,2,1,0:T(8,128)S(1)}, f32[2,1,16,320]{3,2,1,0:T(8,128)S(1)}, u32[]{:S(2)}, u32[]{:S(2)}) %collective-permute-start.16) | collective-permute-done | bytes 40992 | tf_op jit(solution)/shard_map/ppermute | solution.py:13
  171.7 8.0 %collective-permute-start.17 = (f32[2,1,16,320]{3,2,1,0:T(8,128)S(1)}, f32[2,1,16,320]{3,2,1,0:T(8,128)S(1)}, u32[]{:S(2)}, u32[]{:S(2)}) collective-permute-start(f32[2,1,16,320]{3,2,1,0:T(8,128)S(1)} %slice.1332), channel_id=1, source_target_pairs={{0,16},{16,32},{32,48},{48,64},{64,80},{80,96},{96,112},{1,17},{17... | collective-permute-start | bytes 122888 | tf_op jit(solution)/shard_map/ppermute | solution.py:13
  179.7 1.7 collective-permute-done.17
  182.3 1.3 collective-permute-start.18
  184.1 4.5 %collective-permute-done.18 = f32[2,1,16,320]{3,2,1,0:T(8,128)S(1)} collective-permute-done((f32[2,1,16,320]{3,2,1,0:T(8,128)S(1)}, f32[2,1,16,320]{3,2,1,0:T(8,128)S(1)}, u32[]{:S(2)}, u32[]{:S(2)}) %collective-permute-start.18) | collective-permute-done | bytes 40992 | tf_op jit(solution)/shard_map/ppermute | solution.py:13
  189.4 7.5 %collective-permute-start.19 = (f32[2,1,16,320]{3,2,1,0:T(8,128)S(1)}, f32[2,1,16,320]{3,2,1,0:T(8,128)S(1)}, u32[]{:S(2)}, u32[]{:S(2)}) collective-permute-start(f32[2,1,16,320]{3,2,1,0:T(8,128)S(1)} %slice.1356), channel_id=1, source_target_pairs={{0,16},{16,32},{32,48},{48,64},{64,80},{80,96},{96,112},{1,17},{17... | collective-permute-start | bytes 122888 | tf_op jit(solution)/shard_map/ppermute | solution.py:13
  197.0 1.7 collective-permute-done.19
  199.5 1.3 collective-permute-start.20
  201.2 4.5 %collective-permute-done.20 = f32[2,1,16,320]{3,2,1,0:T(8,128)S(1)} collective-permute-done((f32[2,1,16,320]{3,2,1,0:T(8,128)S(1)}, f32[2,1,16,320]{3,2,1,0:T(8,128)S(1)}, u32[]{:S(2)}, u32[]{:S(2)}) %collective-permute-start.20) | collective-permute-done | bytes 40992 | tf_op jit(solution)/shard_map/ppermute | solution.py:13
  206.7 7.5 %collective-permute-start.21 = (f32[2,1,16,320]{3,2,1,0:T(8,128)S(1)}, f32[2,1,16,320]{3,2,1,0:T(8,128)S(1)}, u32[]{:S(2)}, u32[]{:S(2)}) collective-permute-start(f32[2,1,16,320]{3,2,1,0:T(8,128)S(1)} %slice.1380), channel_id=1, source_target_pairs={{0,16},{16,32},{32,48},{48,64},{64,80},{80,96},{96,112},{1,17},{17... | collective-permute-start | bytes 122888 | tf_op jit(solution)/shard_map/ppermute | solution.py:13
  214.3 1.7 collective-permute-done.21
  218.0 3.7 %fusion.6 = f32[1,3,16,16,320]{4,3,2,1,0:T(8,128)} fusion(f32[1,3,16,16,320]{4,3,2,1,0:T(8,128)S(1)} %copy-done, f32[1,1,16,16,320]{4,3,2,1,0:T(8,128)S(1)} %bitcast.800, f32[1,1,16,16,320]{4,3,2,1,0:T(8,128)S(1)} %bitcast.807, f32[1,1,16,16,320]{4,3,2,1,0:T(8,128)S(1)} %bitcast.793, f32[1,1,16,16,320]{4,3,2,1,0:T(8,128)S(1)} %bitcast.819, ...), kind=kLoop, calls=%fused_computation.8 | loop fusion | flops 5898240 | bytes 8192000 | tf_op jit(solution)/shard_map/add | solution.py:70
  221.7 62.3 %reduce-scatter.2.cloned.1.call-done = f32[1,16,320]{2,1,0:T(8,128)} async-done(((f32[16,16,320]{2,1,0:T(8,128)}), f32[1,16,320]{2,1,0:T(8,128)}) %reduce-scatter.2.cloned.1.call-update) | async-done | bytes 20496 | tf_op jit(solution)/shard_map/reduce_scatter | solution.py:57
  284.0 1.4 multiply_divide_fusion
  (216 shorter events, 28.0 us)
Async XLA Ops:
  7.2 276.9 %reduce-scatter.2.cloned.1.call-start = ((), (), s32[]{:S(2)}) async-start(), calls=%async_computation.1 | async-start | bytes 417792 | tf_op jit(solution)/shard_map/reduce_scatter | solution.py:57
  8.0 2.7 copy-start.17
  8.0 25.0 %collective-permute-start = (f32[2,1,16,320]{3,2,1,0:T(8,128)S(1)}, f32[2,1,16,320]{3,2,1,0:T(8,128)S(1)}, u32[]{:S(2)}, u32[]{:S(2)}) collective-permute-start(f32[2,1,16,320]{3,2,1,0:T(8,128)S(1)} %slice.1129), channel_id=1, source_target_pairs={{16,0},{32,16},{48,32},{64,48},{80,64},{96,80},{112,96},{17,1},{33... | collective-permute-start | bytes 122888 | tf_op jit(solution)/shard_map/ppermute | solution.py:13
  10.8 21.8 %copy-start = (f32[1,3,16,16,320]{4,3,2,1,0:T(8,128)S(1)}, f32[1,3,16,16,320]{4,3,2,1,0:T(8,128)}, u32[]{:S(2)}) copy-start(f32[1,3,16,16,320]{4,3,2,1,0:T(8,128)} %param.6) | copy-start | bytes 2949124
  32.6 77.6 %copy-start.3 = (f32[16,16,320]{2,1,0:T(8,128)}, f32[16,16,320]{2,1,0:T(8,128)S(1)}, u32[]{:S(2)}) copy-start(f32[16,16,320]{2,1,0:T(8,128)S(1)} %get-tuple-element.191) | copy-start | bytes 983044
  33.1 1.3 copy-start.1
  34.6 6.3 %collective-permute-start.1 = (f32[2,1,16,320]{3,2,1,0:T(8,128)S(1)}, f32[2,1,16,320]{3,2,1,0:T(8,128)S(1)}, u32[]{:S(2)}, u32[]{:S(2)}) collective-permute-start(f32[2,1,16,320]{3,2,1,0:T(8,128)S(1)} %slice.1140), channel_id=1, source_target_pairs={{0,16},{16,32},{32,48},{48,64},{64,80},{80,96},{96,112},{1,17},{17... | collective-permute-start | bytes 122888 | tf_op jit(solution)/shard_map/ppermute | solution.py:13
  41.7 6.3 %collective-permute-start.2 = (f32[2,1,16,320]{3,2,1,0:T(8,128)S(1)}, f32[2,1,16,320]{3,2,1,0:T(8,128)S(1)}, u32[]{:S(2)}, u32[]{:S(2)}) collective-permute-start(f32[2,1,16,320]{3,2,1,0:T(8,128)S(1)} %slice.1153), channel_id=1, source_target_pairs={{16,0},{32,16},{48,32},{64,48},{80,64},{96,80},{112,96},{17,1},{33... | collective-permute-start | bytes 122888 | tf_op jit(solution)/shard_map/ppermute | solution.py:13
  48.6 5.7 %collective-permute-start.3 = (f32[2,1,16,320]{3,2,1,0:T(8,128)S(1)}, f32[2,1,16,320]{3,2,1,0:T(8,128)S(1)}, u32[]{:S(2)}, u32[]{:S(2)}) collective-permute-start(f32[2,1,16,320]{3,2,1,0:T(8,128)S(1)} %slice.1164), channel_id=1, source_target_pairs={{0,16},{16,32},{32,48},{48,64},{64,80},{80,96},{96,112},{1,17},{17... | collective-permute-start | bytes 122888 | tf_op jit(solution)/shard_map/ppermute | solution.py:13
  55.1 9.3 %collective-permute-start.4 = (f32[2,1,16,320]{3,2,1,0:T(8,128)S(1)}, f32[2,1,16,320]{3,2,1,0:T(8,128)S(1)}, u32[]{:S(2)}, u32[]{:S(2)}) collective-permute-start(f32[2,1,16,320]{3,2,1,0:T(8,128)S(1)} %slice.1177), channel_id=1, source_target_pairs={{16,0},{32,16},{48,32},{64,48},{80,64},{96,80},{112,96},{17,1},{33... | collective-permute-start | bytes 122888 | tf_op jit(solution)/shard_map/ppermute | solution.py:13
  65.2 9.6 %collective-permute-start.5 = (f32[2,1,16,320]{3,2,1,0:T(8,128)S(1)}, f32[2,1,16,320]{3,2,1,0:T(8,128)S(1)}, u32[]{:S(2)}, u32[]{:S(2)}) collective-permute-start(f32[2,1,16,320]{3,2,1,0:T(8,128)S(1)} %slice.1188), channel_id=1, source_target_pairs={{0,16},{16,32},{32,48},{48,64},{64,80},{80,96},{96,112},{1,17},{17... | collective-permute-start | bytes 122888 | tf_op jit(solution)/shard_map/ppermute | solution.py:13
  75.3 141.1 %copy-start.4 = (f32[16,16,320]{2,1,0:T(8,128)}, f32[16,16,320]{2,1,0:T(8,128)S(1)}, u32[]{:S(2)}) copy-start(f32[16,16,320]{2,1,0:T(8,128)S(1)} %get-tuple-element.142) | copy-start | bytes 983044
  75.3 141.1 %copy-start.5 = (f32[16,16,320]{2,1,0:T(8,128)}, f32[16,16,320]{2,1,0:T(8,128)S(1)}, u32[]{:S(2)}) copy-start(f32[16,16,320]{2,1,0:T(8,128)S(1)} %get-tuple-element.143) | copy-start | bytes 983044
  75.3 141.1 %copy-start.6 = (f32[16,16,320]{2,1,0:T(8,128)}, f32[16,16,320]{2,1,0:T(8,128)S(1)}, u32[]{:S(2)}) copy-start(f32[16,16,320]{2,1,0:T(8,128)S(1)} %get-tuple-element.144) | copy-start | bytes 983044
  75.8 6.3 %collective-permute-start.6 = (f32[2,1,16,320]{3,2,1,0:T(8,128)S(1)}, f32[2,1,16,320]{3,2,1,0:T(8,128)S(1)}, u32[]{:S(2)}, u32[]{:S(2)}) collective-permute-start(f32[2,1,16,320]{3,2,1,0:T(8,128)S(1)} %slice.1201), channel_id=1, source_target_pairs={{16,0},{32,16},{48,32},{64,48},{80,64},{96,80},{112,96},{17,1},{33... | collective-permute-start | bytes 122888 | tf_op jit(solution)/shard_map/ppermute | solution.py:13
  82.9 9.3 %collective-permute-start.7 = (f32[2,1,16,320]{3,2,1,0:T(8,128)S(1)}, f32[2,1,16,320]{3,2,1,0:T(8,128)S(1)}, u32[]{:S(2)}, u32[]{:S(2)}) collective-permute-start(f32[2,1,16,320]{3,2,1,0:T(8,128)S(1)} %slice.1212), channel_id=1, source_target_pairs={{0,16},{16,32},{32,48},{48,64},{64,80},{80,96},{96,112},{1,17},{17... | collective-permute-start | bytes 122888 | tf_op jit(solution)/shard_map/ppermute | solution.py:13
  92.6 71.3 %copy-start.7 = (f32[16,16,320]{2,1,0:T(8,128)}, f32[16,16,320]{2,1,0:T(8,128)S(1)}, u32[]{:S(2)}) copy-start(f32[16,16,320]{2,1,0:T(8,128)S(1)} %get-tuple-element.126) | copy-start | bytes 983044
  92.7 71.3 %copy-start.8 = (f32[16,16,320]{2,1,0:T(8,128)}, f32[16,16,320]{2,1,0:T(8,128)S(1)}, u32[]{:S(2)}) copy-start(f32[16,16,320]{2,1,0:T(8,128)S(1)} %get-tuple-element.127) | copy-start | bytes 983044
  92.7 71.3 %copy-start.9 = (f32[16,16,320]{2,1,0:T(8,128)}, f32[16,16,320]{2,1,0:T(8,128)S(1)}, u32[]{:S(2)}) copy-start(f32[16,16,320]{2,1,0:T(8,128)S(1)} %get-tuple-element.128) | copy-start | bytes 983044
  93.2 6.3 %collective-permute-start.8 = (f32[2,1,16,320]{3,2,1,0:T(8,128)S(1)}, f32[2,1,16,320]{3,2,1,0:T(8,128)S(1)}, u32[]{:S(2)}, u32[]{:S(2)}) collective-permute-start(f32[2,1,16,320]{3,2,1,0:T(8,128)S(1)} %slice.1225), channel_id=1, source_target_pairs={{16,0},{32,16},{48,32},{64,48},{80,64},{96,80},{112,96},{17,1},{33... | collective-permute-start | bytes 122888 | tf_op jit(solution)/shard_map/ppermute | solution.py:13
  100.4 9.3 %collective-permute-start.9 = (f32[2,1,16,320]{3,2,1,0:T(8,128)S(1)}, f32[2,1,16,320]{3,2,1,0:T(8,128)S(1)}, u32[]{:S(2)}, u32[]{:S(2)}) collective-permute-start(f32[2,1,16,320]{3,2,1,0:T(8,128)S(1)} %slice.1236), channel_id=1, source_target_pairs={{0,16},{16,32},{32,48},{48,64},{64,80},{80,96},{96,112},{1,17},{17... | collective-permute-start | bytes 122888 | tf_op jit(solution)/shard_map/ppermute | solution.py:13
  110.1 53.8 %copy-start.10 = (f32[16,16,320]{2,1,0:T(8,128)}, f32[16,16,320]{2,1,0:T(8,128)S(1)}, u32[]{:S(2)}) copy-start(f32[16,16,320]{2,1,0:T(8,128)S(1)} %get-tuple-element.110) | copy-start | bytes 983044
  110.1 53.8 %copy-start.11 = (f32[16,16,320]{2,1,0:T(8,128)}, f32[16,16,320]{2,1,0:T(8,128)S(1)}, u32[]{:S(2)}) copy-start(f32[16,16,320]{2,1,0:T(8,128)S(1)} %get-tuple-element.111) | copy-start | bytes 983044
  110.1 53.8 %copy-start.12 = (f32[16,16,320]{2,1,0:T(8,128)}, f32[16,16,320]{2,1,0:T(8,128)S(1)}, u32[]{:S(2)}) copy-start(f32[16,16,320]{2,1,0:T(8,128)S(1)} %get-tuple-element.112) | copy-start | bytes 983044
  110.8 6.3 %collective-permute-start.10 = (f32[2,1,16,320]{3,2,1,0:T(8,128)S(1)}, f32[2,1,16,320]{3,2,1,0:T(8,128)S(1)}, u32[]{:S(2)}, u32[]{:S(2)}) collective-permute-start(f32[2,1,16,320]{3,2,1,0:T(8,128)S(1)} %slice.1249), channel_id=1, source_target_pairs={{16,0},{32,16},{48,32},{64,48},{80,64},{96,80},{112,96},{17,1},{33... | collective-permute-start | bytes 122888 | tf_op jit(solution)/shard_map/ppermute | solution.py:13
  118.2 9.3 %collective-permute-start.11 = (f32[2,1,16,320]{3,2,1,0:T(8,128)S(1)}, f32[2,1,16,320]{3,2,1,0:T(8,128)S(1)}, u32[]{:S(2)}, u32[]{:S(2)}) collective-permute-start(f32[2,1,16,320]{3,2,1,0:T(8,128)S(1)} %slice.1260), channel_id=1, source_target_pairs={{0,16},{16,32},{32,48},{48,64},{64,80},{80,96},{96,112},{1,17},{17... | collective-permute-start | bytes 122888 | tf_op jit(solution)/shard_map/ppermute | solution.py:13
  127.5 1.3 copy-start.13
  128.0 1.0 copy-start.14
  128.0 1.0 copy-start.15
  128.0 1.0 copy-start.16
  129.1 6.3 %collective-permute-start.12 = (f32[2,1,16,320]{3,2,1,0:T(8,128)S(1)}, f32[2,1,16,320]{3,2,1,0:T(8,128)S(1)}, u32[]{:S(2)}, u32[]{:S(2)}) collective-permute-start(f32[2,1,16,320]{3,2,1,0:T(8,128)S(1)} %slice.1273), channel_id=1, source_target_pairs={{16,0},{32,16},{48,32},{64,48},{80,64},{96,80},{112,96},{17,1},{33... | collective-permute-start | bytes 122888 | tf_op jit(solution)/shard_map/ppermute | solution.py:13
  135.4 1.3 copy-start.2
  137.0 9.3 %collective-permute-start.13 = (f32[2,1,16,320]{3,2,1,0:T(8,128)S(1)}, f32[2,1,16,320]{3,2,1,0:T(8,128)S(1)}, u32[]{:S(2)}, u32[]{:S(2)}) collective-permute-start(f32[2,1,16,320]{3,2,1,0:T(8,128)S(1)} %slice.1284), channel_id=1, source_target_pairs={{0,16},{16,32},{32,48},{48,64},{64,80},{80,96},{96,112},{1,17},{17... | collective-permute-start | bytes 122888 | tf_op jit(solution)/shard_map/ppermute | solution.py:13
  147.1 6.3 %collective-permute-start.14 = (f32[2,1,16,320]{3,2,1,0:T(8,128)S(1)}, f32[2,1,16,320]{3,2,1,0:T(8,128)S(1)}, u32[]{:S(2)}, u32[]{:S(2)}) collective-permute-start(f32[2,1,16,320]{3,2,1,0:T(8,128)S(1)} %slice.1297), channel_id=1, source_target_pairs={{16,0},{32,16},{48,32},{64,48},{80,64},{96,80},{112,96},{17,1},{33... | collective-permute-start | bytes 122888 | tf_op jit(solution)/shard_map/ppermute | solution.py:13
  154.1 9.3 %collective-permute-start.15 = (f32[2,1,16,320]{3,2,1,0:T(8,128)S(1)}, f32[2,1,16,320]{3,2,1,0:T(8,128)S(1)}, u32[]{:S(2)}, u32[]{:S(2)}) collective-permute-start(f32[2,1,16,320]{3,2,1,0:T(8,128)S(1)} %slice.1308), channel_id=1, source_target_pairs={{0,16},{16,32},{32,48},{48,64},{64,80},{80,96},{96,112},{1,17},{17... | collective-permute-start | bytes 122888 | tf_op jit(solution)/shard_map/ppermute | solution.py:13
  164.5 6.5 %collective-permute-start.16 = (f32[2,1,16,320]{3,2,1,0:T(8,128)S(1)}, f32[2,1,16,320]{3,2,1,0:T(8,128)S(1)}, u32[]{:S(2)}, u32[]{:S(2)}) collective-permute-start(f32[2,1,16,320]{3,2,1,0:T(8,128)S(1)} %slice.1321), channel_id=1, source_target_pairs={{16,0},{32,16},{48,32},{64,48},{80,64},{96,80},{112,96},{17,1},{33... | collective-permute-start | bytes 122888 | tf_op jit(solution)/shard_map/ppermute | solution.py:13
  171.7 9.7 %collective-permute-start.17 = (f32[2,1,16,320]{3,2,1,0:T(8,128)S(1)}, f32[2,1,16,320]{3,2,1,0:T(8,128)S(1)}, u32[]{:S(2)}, u32[]{:S(2)}) collective-permute-start(f32[2,1,16,320]{3,2,1,0:T(8,128)S(1)} %slice.1332), channel_id=1, source_target_pairs={{0,16},{16,32},{32,48},{48,64},{64,80},{80,96},{96,112},{1,17},{17... | collective-permute-start | bytes 122888 | tf_op jit(solution)/shard_map/ppermute | solution.py:13
  182.3 6.3 %collective-permute-start.18 = (f32[2,1,16,320]{3,2,1,0:T(8,128)S(1)}, f32[2,1,16,320]{3,2,1,0:T(8,128)S(1)}, u32[]{:S(2)}, u32[]{:S(2)}) collective-permute-start(f32[2,1,16,320]{3,2,1,0:T(8,128)S(1)} %slice.1345), channel_id=1, source_target_pairs={{16,0},{32,16},{48,32},{64,48},{80,64},{96,80},{112,96},{17,1},{33... | collective-permute-start | bytes 122888 | tf_op jit(solution)/shard_map/ppermute | solution.py:13
  189.4 9.3 %collective-permute-start.19 = (f32[2,1,16,320]{3,2,1,0:T(8,128)S(1)}, f32[2,1,16,320]{3,2,1,0:T(8,128)S(1)}, u32[]{:S(2)}, u32[]{:S(2)}) collective-permute-start(f32[2,1,16,320]{3,2,1,0:T(8,128)S(1)} %slice.1356), channel_id=1, source_target_pairs={{0,16},{16,32},{32,48},{48,64},{64,80},{80,96},{96,112},{1,17},{17... | collective-permute-start | bytes 122888 | tf_op jit(solution)/shard_map/ppermute | solution.py:13
  199.5 6.3 %collective-permute-start.20 = (f32[2,1,16,320]{3,2,1,0:T(8,128)S(1)}, f32[2,1,16,320]{3,2,1,0:T(8,128)S(1)}, u32[]{:S(2)}, u32[]{:S(2)}) collective-permute-start(f32[2,1,16,320]{3,2,1,0:T(8,128)S(1)} %slice.1369), channel_id=1, source_target_pairs={{16,0},{32,16},{48,32},{64,48},{80,64},{96,80},{112,96},{17,1},{33... | collective-permute-start | bytes 122888 | tf_op jit(solution)/shard_map/ppermute | solution.py:13
  206.7 9.3 %collective-permute-start.21 = (f32[2,1,16,320]{3,2,1,0:T(8,128)S(1)}, f32[2,1,16,320]{3,2,1,0:T(8,128)S(1)}, u32[]{:S(2)}, u32[]{:S(2)}) collective-permute-start(f32[2,1,16,320]{3,2,1,0:T(8,128)S(1)} %slice.1380), channel_id=1, source_target_pairs={{0,16},{16,32},{32,48},{48,64},{64,80},{80,96},{96,112},{1,17},{17... | collective-permute-start | bytes 122888 | tf_op jit(solution)/shard_map/ppermute | solution.py:13
Sparse Core Ops, SparseCore 0:
  218.2 65.8 reduce-scatter.1
where the time goes:
time: 293 us; the launch traced here: 292 us
  waiting for transfers between devices  129 us (44%)
  starting transfers between devices  91.6 us (31%)
  other arithmetic  22 us (8%)
  blocking collectives  21.7 us (7%)
  between operations  15.5 us (5%)
  local copies, waits for them, and re-layouts  12.3 us (4%)
    ppermute x22, starting transfers between devices, passed_along(): return lax.ppermute(array, axis, pairs)  91.6 us
    ppermute x22, waiting for transfers between devices, passed_along(): return lax.ppermute(array, axis, pairs)  66.7 us
    reduce_scatter x1, waiting for transfers between devices, add_term(): lax.psum_scatter(term, 'src', scatter_dimension=0, tiled=True)  62.3 us
    all_gather x1, blocking collectives, on_device(): window = lax.all_gather(permittivity, 'src', axis=0, tiled=True)  21.7 us
  transfers between devices with their start and end apart: 23, of which 22 were waited for; matrix products, arithmetic and copies ran while one was open for 4% of the time, Pallas kernels for 0%

commit v1 on v0

--- a/solution.py
+++ b/solution.py
@@ -59,7 +59,9 @@
 
 
 def on_device(permittivity, e_start, h_start, e_cotangent, h_cotangent):
-    window = lax.all_gather(permittivity, "src", axis=0, tiled=True)
+    window = jnp.concatenate(
+        lax.all_to_all(jnp.stack([permittivity] * lax.axis_size("src")), "src", 0, 0), axis=0
+    )
     inverse = 1.0 / window
     efield = e_start[0]
     hfield = h_start[0]

time: 293 us -> 283 us (0.966)
  blocking collectives: 21.7 us -> 0 us
  starting transfers between devices: 91.6 us -> 97.1 us
    all_gather x1 -> x0, blocking collectives: 21.7 us -> none  [on_device(): window = lax.all_gather(permittivity, 'src', axis=0, tiled=True)]
    all_to_all x0 -> x1, starting transfers between devices: none -> 5.66 us  [on_device(): lax.all_to_all(jnp.stack([permittivity] * lax.axis_size('src')), 'src', 0...]
  transfers between devices with their start and end apart: 23 -> 24, of which waited for: 22 -> 23; matrix products, arithmetic and copies ran while one was open for 4% -> 4% of each run, Pallas kernels for 0% -> 0%
where the time goes in v1:
time: 283 us; the launch traced here: 282 us
  waiting for transfers between devices  131 us (46%)
  starting transfers between devices  97.1 us (34%)
  other arithmetic  24 us (8%)
  between operations  15.7 us (6%)
  local copies, waits for them, and re-layouts  14.2 us (5%)
    ppermute x22, starting transfers between devices, passed_along(): return lax.ppermute(array, axis, pairs)  91.4 us
    ppermute x22, waiting for transfers between devices, passed_along(): return lax.ppermute(array, axis, pairs)  65.4 us
    reduce_scatter x1, waiting for transfers between devices, add_term(): lax.psum_scatter(term, 'src', scatter_dimension=0, tiled=True)  64.9 us
  transfers between devices with their start and end apart: 24, of which 23 were waited for; matrix products, arithmetic and copies ran while one was open for 4% of the time, Pallas kernels for 0%

profile of v1, /device:TPU:0, one launch (start us, length us, event | category | flops | bytes accessed | tf_op | source)
XLA Modules:
  0.0 281.7 jit_solution(14012545013130391032)
XLA Ops:
  8.1 1.3 collective-permute-start
  9.4 1.5 stack.331
  10.9 5.7 %all-to-all-start = ((f32[16,1,16,320]{3,2,1,0:T(8,128)}), f32[16,1,16,320]{3,2,1,0:T(8,128)}, u32[]{:S(2)}, u32[]{:S(2)}) async-start(f32[16,1,16,320]{3,2,1,0:T(8,128)} %stack.331), calls=%async_computation | async-start | bytes 786432 | tf_op jit(solution)/shard_map/all_to_all | solution.py:63
  18.9 4.5 %collective-permute-start.1 = (f32[2,1,16,320]{3,2,1,0:T(8,128)S(1)}, f32[2,1,16,320]{3,2,1,0:T(8,128)S(1)}, u32[]{:S(2)}, u32[]{:S(2)}) collective-permute-start(f32[2,1,16,320]{3,2,1,0:T(8,128)S(1)} %slice.1140), channel_id=1, source_target_pairs={{0,16},{16,32},{32,48},{48,64},{64,80},{80,96},{96,112},{1,17},{17... | collective-permute-start | bytes 122888 | tf_op jit(solution)/shard_map/ppermute | solution.py:13
  23.5 1.7 collective-permute-done.1
  27.4 1.3 collective-permute-start.2
  30.2 3.8 %collective-permute-done.2 = f32[2,1,16,320]{3,2,1,0:T(8,128)S(1)} collective-permute-done((f32[2,1,16,320]{3,2,1,0:T(8,128)S(1)}, f32[2,1,16,320]{3,2,1,0:T(8,128)S(1)}, u32[]{:S(2)}, u32[]{:S(2)}) %collective-permute-start.2) | collective-permute-done | bytes 40992 | tf_op jit(solution)/shard_map/ppermute | solution.py:13
  35.6 3.9 %collective-permute-start.3 = (f32[2,1,16,320]{3,2,1,0:T(8,128)S(1)}, f32[2,1,16,320]{3,2,1,0:T(8,128)S(1)}, u32[]{:S(2)}, u32[]{:S(2)}) collective-permute-start(f32[2,1,16,320]{3,2,1,0:T(8,128)S(1)} %slice.1164), channel_id=1, source_target_pairs={{0,16},{16,32},{32,48},{48,64},{64,80},{80,96},{96,112},{1,17},{17... | collective-permute-start | bytes 122888 | tf_op jit(solution)/shard_map/ppermute | solution.py:13
  39.6 1.7 collective-permute-done.3
  42.2 1.3 collective-permute-start.4
  44.0 6.9 %collective-permute-done.4 = f32[2,1,16,320]{3,2,1,0:T(8,128)S(1)} collective-permute-done((f32[2,1,16,320]{3,2,1,0:T(8,128)S(1)}, f32[2,1,16,320]{3,2,1,0:T(8,128)S(1)}, u32[]{:S(2)}, u32[]{:S(2)}) %collective-permute-start.4) | collective-permute-done | bytes 40992 | tf_op jit(solution)/shard_map/ppermute | solution.py:13
  51.6 7.9 %collective-permute-start.5 = (f32[2,1,16,320]{3,2,1,0:T(8,128)S(1)}, f32[2,1,16,320]{3,2,1,0:T(8,128)S(1)}, u32[]{:S(2)}, u32[]{:S(2)}) collective-permute-start(f32[2,1,16,320]{3,2,1,0:T(8,128)S(1)} %slice.1188), channel_id=1, source_target_pairs={{0,16},{16,32},{32,48},{48,64},{64,80},{80,96},{96,112},{1,17},{17... | collective-permute-start | bytes 122888 | tf_op jit(solution)/shard_map/ppermute | solution.py:13
  59.6 1.7 collective-permute-done.5
  62.2 1.3 collective-permute-start.6
  64.0 4.5 %collective-permute-done.6 = f32[2,1,16,320]{3,2,1,0:T(8,128)S(1)} collective-permute-done((f32[2,1,16,320]{3,2,1,0:T(8,128)S(1)}, f32[2,1,16,320]{3,2,1,0:T(8,128)S(1)}, u32[]{:S(2)}, u32[]{:S(2)}) %collective-permute-start.6) | collective-permute-done | bytes 40992 | tf_op jit(solution)/shard_map/ppermute | solution.py:13
  69.3 7.5 %collective-permute-start.7 = (f32[2,1,16,320]{3,2,1,0:T(8,128)S(1)}, f32[2,1,16,320]{3,2,1,0:T(8,128)S(1)}, u32[]{:S(2)}, u32[]{:S(2)}) collective-permute-start(f32[2,1,16,320]{3,2,1,0:T(8,128)S(1)} %slice.1212), channel_id=1, source_target_pairs={{0,16},{16,32},{32,48},{48,64},{64,80},{80,96},{96,112},{1,17},{17... | collective-permute-start | bytes 122888 | tf_op jit(solution)/shard_map/ppermute | solution.py:13
  76.9 1.7 collective-permute-done.7
  79.7 1.3 collective-permute-start.8
  81.4 4.5 %collective-permute-done.8 = f32[2,1,16,320]{3,2,1,0:T(8,128)S(1)} collective-permute-done((f32[2,1,16,320]{3,2,1,0:T(8,128)S(1)}, f32[2,1,16,320]{3,2,1,0:T(8,128)S(1)}, u32[]{:S(2)}, u32[]{:S(2)}) %collective-permute-start.8) | collective-permute-done | bytes 40992 | tf_op jit(solution)/shard_map/ppermute | solution.py:13
  86.9 7.5 %collective-permute-start.9 = (f32[2,1,16,320]{3,2,1,0:T(8,128)S(1)}, f32[2,1,16,320]{3,2,1,0:T(8,128)S(1)}, u32[]{:S(2)}, u32[]{:S(2)}) collective-permute-start(f32[2,1,16,320]{3,2,1,0:T(8,128)S(1)} %slice.1236), channel_id=1, source_target_pairs={{0,16},{16,32},{32,48},{48,64},{64,80},{80,96},{96,112},{1,17},{17... | collective-permute-start | bytes 122888 | tf_op jit(solution)/shard_map/ppermute | solution.py:13
  94.5 1.7 collective-permute-done.9
  97.3 1.5 collective-permute-start.10
  99.2 4.4 %collective-permute-done.10 = f32[2,1,16,320]{3,2,1,0:T(8,128)S(1)} collective-permute-done((f32[2,1,16,320]{3,2,1,0:T(8,128)S(1)}, f32[2,1,16,320]{3,2,1,0:T(8,128)S(1)}, u32[]{:S(2)}, u32[]{:S(2)}) %collective-permute-start.10) | collective-permute-done | bytes 40992 | tf_op jit(solution)/shard_map/ppermute | solution.py:13
  104.6 7.5 %collective-permute-start.11 = (f32[2,1,16,320]{3,2,1,0:T(8,128)S(1)}, f32[2,1,16,320]{3,2,1,0:T(8,128)S(1)}, u32[]{:S(2)}, u32[]{:S(2)}) collective-permute-start(f32[2,1,16,320]{3,2,1,0:T(8,128)S(1)} %slice.1260), channel_id=1, source_target_pairs={{0,16},{16,32},{32,48},{48,64},{64,80},{80,96},{96,112},{1,17},{17... | collective-permute-start | bytes 122888 | tf_op jit(solution)/shard_map/ppermute | solution.py:13
  112.2 1.7 collective-permute-done.11
  115.5 1.3 collective-permute-start.12
  117.3 4.5 %collective-permute-done.12 = f32[2,1,16,320]{3,2,1,0:T(8,128)S(1)} collective-permute-done((f32[2,1,16,320]{3,2,1,0:T(8,128)S(1)}, f32[2,1,16,320]{3,2,1,0:T(8,128)S(1)}, u32[]{:S(2)}, u32[]{:S(2)}) %collective-permute-start.12) | collective-permute-done | bytes 40992 | tf_op jit(solution)/shard_map/ppermute | solution.py:13
  123.4 7.5 %collective-permute-start.13 = (f32[2,1,16,320]{3,2,1,0:T(8,128)S(1)}, f32[2,1,16,320]{3,2,1,0:T(8,128)S(1)}, u32[]{:S(2)}, u32[]{:S(2)}) collective-permute-start(f32[2,1,16,320]{3,2,1,0:T(8,128)S(1)} %slice.1284), channel_id=1, source_target_pairs={{0,16},{16,32},{32,48},{48,64},{64,80},{80,96},{96,112},{1,17},{17... | collective-permute-start | bytes 122888 | tf_op jit(solution)/shard_map/ppermute | solution.py:13
  131.0 1.7 collective-permute-done.13
  133.5 1.3 collective-permute-start.14
  135.3 4.5 %collective-permute-done.14 = f32[2,1,16,320]{3,2,1,0:T(8,128)S(1)} collective-permute-done((f32[2,1,16,320]{3,2,1,0:T(8,128)S(1)}, f32[2,1,16,320]{3,2,1,0:T(8,128)S(1)}, u32[]{:S(2)}, u32[]{:S(2)}) %collective-permute-start.14) | collective-permute-done | bytes 40992 | tf_op jit(solution)/shard_map/ppermute | solution.py:13
  140.5 7.5 %collective-permute-start.15 = (f32[2,1,16,320]{3,2,1,0:T(8,128)S(1)}, f32[2,1,16,320]{3,2,1,0:T(8,128)S(1)}, u32[]{:S(2)}, u32[]{:S(2)}) collective-permute-start(f32[2,1,16,320]{3,2,1,0:T(8,128)S(1)} %slice.1308), channel_id=1, source_target_pairs={{0,16},{16,32},{32,48},{48,64},{64,80},{80,96},{96,112},{1,17},{17... | collective-permute-start | bytes 122888 | tf_op jit(solution)/shard_map/ppermute | solution.py:13
  148.1 1.7 collective-permute-done.15
  150.9 1.3 collective-permute-start.16
  152.7 4.7 %collective-permute-done.16 = f32[2,1,16,320]{3,2,1,0:T(8,128)S(1)} collective-permute-done((f32[2,1,16,320]{3,2,1,0:T(8,128)S(1)}, f32[2,1,16,320]{3,2,1,0:T(8,128)S(1)}, u32[]{:S(2)}, u32[]{:S(2)}) %collective-permute-start.16) | collective-permute-done | bytes 40992 | tf_op jit(solution)/shard_map/ppermute | solution.py:13
  158.1 8.0 %collective-permute-start.17 = (f32[2,1,16,320]{3,2,1,0:T(8,128)S(1)}, f32[2,1,16,320]{3,2,1,0:T(8,128)S(1)}, u32[]{:S(2)}, u32[]{:S(2)}) collective-permute-start(f32[2,1,16,320]{3,2,1,0:T(8,128)S(1)} %slice.1332), channel_id=1, source_target_pairs={{0,16},{16,32},{32,48},{48,64},{64,80},{80,96},{96,112},{1,17},{17... | collective-permute-start | bytes 122888 | tf_op jit(solution)/shard_map/ppermute | solution.py:13
  166.1 1.7 collective-permute-done.17
  168.7 1.3 collective-permute-start.18
  170.5 4.5 %collective-permute-done.18 = f32[2,1,16,320]{3,2,1,0:T(8,128)S(1)} collective-permute-done((f32[2,1,16,320]{3,2,1,0:T(8,128)S(1)}, f32[2,1,16,320]{3,2,1,0:T(8,128)S(1)}, u32[]{:S(2)}, u32[]{:S(2)}) %collective-permute-start.18) | collective-permute-done | bytes 40992 | tf_op jit(solution)/shard_map/ppermute | solution.py:13
  175.8 7.5 %collective-permute-start.19 = (f32[2,1,16,320]{3,2,1,0:T(8,128)S(1)}, f32[2,1,16,320]{3,2,1,0:T(8,128)S(1)}, u32[]{:S(2)}, u32[]{:S(2)}) collective-permute-start(f32[2,1,16,320]{3,2,1,0:T(8,128)S(1)} %slice.1356), channel_id=1, source_target_pairs={{0,16},{16,32},{32,48},{48,64},{64,80},{80,96},{96,112},{1,17},{17... | collective-permute-start | bytes 122888 | tf_op jit(solution)/shard_map/ppermute | solution.py:13
  183.4 1.7 collective-permute-done.19
  185.9 1.3 collective-permute-start.20
  187.6 4.5 %collective-permute-done.20 = f32[2,1,16,320]{3,2,1,0:T(8,128)S(1)} collective-permute-done((f32[2,1,16,320]{3,2,1,0:T(8,128)S(1)}, f32[2,1,16,320]{3,2,1,0:T(8,128)S(1)}, u32[]{:S(2)}, u32[]{:S(2)}) %collective-permute-start.20) | collective-permute-done | bytes 40992 | tf_op jit(solution)/shard_map/ppermute | solution.py:13
  193.1 7.5 %collective-permute-start.21 = (f32[2,1,16,320]{3,2,1,0:T(8,128)S(1)}, f32[2,1,16,320]{3,2,1,0:T(8,128)S(1)}, u32[]{:S(2)}, u32[]{:S(2)}) collective-permute-start(f32[2,1,16,320]{3,2,1,0:T(8,128)S(1)} %slice.1380), channel_id=1, source_target_pairs={{0,16},{16,32},{32,48},{48,64},{64,80},{80,96},{96,112},{1,17},{17... | collective-permute-start | bytes 122888 | tf_op jit(solution)/shard_map/ppermute | solution.py:13
  200.7 1.7 collective-permute-done.21
  204.9 3.7 %fusion.6 = f32[1,3,16,16,320]{4,3,2,1,0:T(8,128)} fusion(f32[1,3,16,16,320]{4,3,2,1,0:T(8,128)S(1)} %copy-done, f32[1,1,16,16,320]{4,3,2,1,0:T(8,128)S(1)} %bitcast.805, f32[1,1,16,16,320]{4,3,2,1,0:T(8,128)S(1)} %bitcast.812, f32[1,1,16,16,320]{4,3,2,1,0:T(8,128)S(1)} %bitcast.798, f32[1,1,16,16,320]{4,3,2,1,0:T(8,128)S(1)} %bitcast.824, ...), kind=kLoop, calls=%fused_computation.8 | loop fusion | flops 5898240 | bytes 8192000 | tf_op jit(solution)/shard_map/add | solution.py:72
  208.6 64.9 %reduce-scatter.2.cloned.1.call-done = f32[1,16,320]{2,1,0:T(8,128)} async-done(((f32[16,16,320]{2,1,0:T(8,128)}), f32[1,16,320]{2,1,0:T(8,128)}) %reduce-scatter.2.cloned.1.call-update) | async-done | bytes 20496 | tf_op jit(solution)/shard_map/reduce_scatter | solution.py:57
  273.5 1.4 multiply_divide_fusion
  (241 shorter events, 32.1 us)
Async XLA Ops:
  7.2 9.4 %copy-start = (f32[1,3,16,16,320]{4,3,2,1,0:T(8,128)S(1)}, f32[1,3,16,16,320]{4,3,2,1,0:T(8,128)}, u32[]{:S(2)}) copy-start(f32[1,3,16,16,320]{4,3,2,1,0:T(8,128)} %param.6) | copy-start | bytes 2949124
  8.1 9.1 %collective-permute-start = (f32[2,1,16,320]{3,2,1,0:T(8,128)S(1)}, f32[2,1,16,320]{3,2,1,0:T(8,128)S(1)}, u32[]{:S(2)}, u32[]{:S(2)}) collective-permute-start(f32[2,1,16,320]{3,2,1,0:T(8,128)S(1)} %slice.1129), channel_id=1, source_target_pairs={{16,0},{32,16},{48,32},{64,48},{80,64},{96,80},{112,96},{17,1},{33... | collective-permute-start | bytes 122888 | tf_op jit(solution)/shard_map/ppermute | solution.py:13
  10.9 15.1 %all-to-all-start = ((f32[16,1,16,320]{3,2,1,0:T(8,128)}), f32[16,1,16,320]{3,2,1,0:T(8,128)}, u32[]{:S(2)}, u32[]{:S(2)}) async-start(f32[16,1,16,320]{3,2,1,0:T(8,128)} %stack.331), calls=%async_computation | async-start | bytes 786432 | tf_op jit(solution)/shard_map/all_to_all | solution.py:63
  16.5 257.0 %reduce-scatter.2.cloned.1.call-start = ((), (), s32[]{:S(2)}) async-start(), calls=%async_computation.2 | async-start | bytes 417792 | tf_op jit(solution)/shard_map/reduce_scatter | solution.py:57
  17.2 1.4 copy-start.1
  17.5 1.3 copy-start.10
  17.5 1.3 copy-start.12
  17.5 1.3 copy-start.14
  18.9 6.3 %collective-permute-start.1 = (f32[2,1,16,320]{3,2,1,0:T(8,128)S(1)}, f32[2,1,16,320]{3,2,1,0:T(8,128)S(1)}, u32[]{:S(2)}, u32[]{:S(2)}) collective-permute-start(f32[2,1,16,320]{3,2,1,0:T(8,128)S(1)} %slice.1140), channel_id=1, source_target_pairs={{0,16},{16,32},{32,48},{48,64},{64,80},{80,96},{96,112},{1,17},{17... | collective-permute-start | bytes 122888 | tf_op jit(solution)/shard_map/ppermute | solution.py:13
  27.1 69.5 %copy-start.9 = (f32[16,16,320]{2,1,0:T(8,128)}, f32[16,16,320]{2,1,0:T(8,128)S(1)}, u32[]{:S(2)}) copy-start(f32[16,16,320]{2,1,0:T(8,128)S(1)} %broadcast_multiply_fusion.4) | copy-start | bytes 983044
  27.4 6.6 %collective-permute-start.2 = (f32[2,1,16,320]{3,2,1,0:T(8,128)S(1)}, f32[2,1,16,320]{3,2,1,0:T(8,128)S(1)}, u32[]{:S(2)}, u32[]{:S(2)}) collective-permute-start(f32[2,1,16,320]{3,2,1,0:T(8,128)S(1)} %slice.1153), channel_id=1, source_target_pairs={{16,0},{32,16},{48,32},{64,48},{80,64},{96,80},{112,96},{17,1},{33... | collective-permute-start | bytes 122888 | tf_op jit(solution)/shard_map/ppermute | solution.py:13
  34.0 1.1 copy-start.13
  34.1 1.2 copy-start.15
  35.6 5.7 %collective-permute-start.3 = (f32[2,1,16,320]{3,2,1,0:T(8,128)S(1)}, f32[2,1,16,320]{3,2,1,0:T(8,128)S(1)}, u32[]{:S(2)}, u32[]{:S(2)}) collective-permute-start(f32[2,1,16,320]{3,2,1,0:T(8,128)S(1)} %slice.1164), channel_id=1, source_target_pairs={{0,16},{16,32},{32,48},{48,64},{64,80},{80,96},{96,112},{1,17},{17... | collective-permute-start | bytes 122888 | tf_op jit(solution)/shard_map/ppermute | solution.py:13
  41.8 161.0 %copy-start.3 = (f32[16,16,320]{2,1,0:T(8,128)}, f32[16,16,320]{2,1,0:T(8,128)S(1)}, u32[]{:S(2)}) copy-start(f32[16,16,320]{2,1,0:T(8,128)S(1)} %get-tuple-element.158) | copy-start | bytes 983044
  41.8 161.0 %copy-start.5 = (f32[16,16,320]{2,1,0:T(8,128)}, f32[16,16,320]{2,1,0:T(8,128)S(1)}, u32[]{:S(2)}) copy-start(f32[16,16,320]{2,1,0:T(8,128)S(1)} %get-tuple-element.159) | copy-start | bytes 983044
  41.8 161.0 %copy-start.7 = (f32[16,16,320]{2,1,0:T(8,128)}, f32[16,16,320]{2,1,0:T(8,128)S(1)}, u32[]{:S(2)}) copy-start(f32[16,16,320]{2,1,0:T(8,128)S(1)} %get-tuple-element.160) | copy-start | bytes 983044
  42.2 8.7 %collective-permute-start.4 = (f32[2,1,16,320]{3,2,1,0:T(8,128)S(1)}, f32[2,1,16,320]{3,2,1,0:T(8,128)S(1)}, u32[]{:S(2)}, u32[]{:S(2)}) collective-permute-start(f32[2,1,16,320]{3,2,1,0:T(8,128)S(1)} %slice.1177), channel_id=1, source_target_pairs={{16,0},{32,16},{48,32},{64,48},{80,64},{96,80},{112,96},{17,1},{33... | collective-permute-start | bytes 122888 | tf_op jit(solution)/shard_map/ppermute | solution.py:13
  51.6 9.6 %collective-permute-start.5 = (f32[2,1,16,320]{3,2,1,0:T(8,128)S(1)}, f32[2,1,16,320]{3,2,1,0:T(8,128)S(1)}, u32[]{:S(2)}, u32[]{:S(2)}) collective-permute-start(f32[2,1,16,320]{3,2,1,0:T(8,128)S(1)} %slice.1188), channel_id=1, source_target_pairs={{0,16},{16,32},{32,48},{48,64},{64,80},{80,96},{96,112},{1,17},{17... | collective-permute-start | bytes 122888 | tf_op jit(solution)/shard_map/ppermute | solution.py:13
  61.7 141.1 %copy-start.16 = (f32[16,16,320]{2,1,0:T(8,128)}, f32[16,16,320]{2,1,0:T(8,128)S(1)}, u32[]{:S(2)}) copy-start(f32[16,16,320]{2,1,0:T(8,128)S(1)} %get-tuple-element.142) | copy-start | bytes 983044
  61.7 141.1 %copy-start.17 = (f32[16,16,320]{2,1,0:T(8,128)}, f32[16,16,320]{2,1,0:T(8,128)S(1)}, u32[]{:S(2)}) copy-start(f32[16,16,320]{2,1,0:T(8,128)S(1)} %get-tuple-element.143) | copy-start | bytes 983044
  61.8 141.1 %copy-start.18 = (f32[16,16,320]{2,1,0:T(8,128)}, f32[16,16,320]{2,1,0:T(8,128)S(1)}, u32[]{:S(2)}) copy-start(f32[16,16,320]{2,1,0:T(8,128)S(1)} %get-tuple-element.144) | copy-start | bytes 983044
  62.2 6.3 %collective-permute-start.6 = (f32[2,1,16,320]{3,2,1,0:T(8,128)S(1)}, f32[2,1,16,320]{3,2,1,0:T(8,128)S(1)}, u32[]{:S(2)}, u32[]{:S(2)}) collective-permute-start(f32[2,1,16,320]{3,2,1,0:T(8,128)S(1)} %slice.1201), channel_id=1, source_target_pairs={{16,0},{32,16},{48,32},{64,48},{80,64},{96,80},{112,96},{17,1},{33... | collective-permute-start | bytes 122888 | tf_op jit(solution)/shard_map/ppermute | solution.py:13
  69.3 9.3 %collective-permute-start.7 = (f32[2,1,16,320]{3,2,1,0:T(8,128)S(1)}, f32[2,1,16,320]{3,2,1,0:T(8,128)S(1)}, u32[]{:S(2)}, u32[]{:S(2)}) collective-permute-start(f32[2,1,16,320]{3,2,1,0:T(8,128)S(1)} %slice.1212), channel_id=1, source_target_pairs={{0,16},{16,32},{32,48},{48,64},{64,80},{80,96},{96,112},{1,17},{17... | collective-permute-start | bytes 122888 | tf_op jit(solution)/shard_map/ppermute | solution.py:13
  79.1 71.2 %copy-start.19 = (f32[16,16,320]{2,1,0:T(8,128)}, f32[16,16,320]{2,1,0:T(8,128)S(1)}, u32[]{:S(2)}) copy-start(f32[16,16,320]{2,1,0:T(8,128)S(1)} %get-tuple-element.126) | copy-start | bytes 983044
  79.1 71.2 %copy-start.20 = (f32[16,16,320]{2,1,0:T(8,128)}, f32[16,16,320]{2,1,0:T(8,128)S(1)}, u32[]{:S(2)}) copy-start(f32[16,16,320]{2,1,0:T(8,128)S(1)} %get-tuple-element.127) | copy-start | bytes 983044
  79.1 71.2 %copy-start.21 = (f32[16,16,320]{2,1,0:T(8,128)}, f32[16,16,320]{2,1,0:T(8,128)S(1)}, u32[]{:S(2)}) copy-start(f32[16,16,320]{2,1,0:T(8,128)S(1)} %get-tuple-element.128) | copy-start | bytes 983044
  79.7 6.3 %collective-permute-start.8 = (f32[2,1,16,320]{3,2,1,0:T(8,128)S(1)}, f32[2,1,16,320]{3,2,1,0:T(8,128)S(1)}, u32[]{:S(2)}, u32[]{:S(2)}) collective-permute-start(f32[2,1,16,320]{3,2,1,0:T(8,128)S(1)} %slice.1225), channel_id=1, source_target_pairs={{16,0},{32,16},{48,32},{64,48},{80,64},{96,80},{112,96},{17,1},{33... | collective-permute-start | bytes 122888 | tf_op jit(solution)/shard_map/ppermute | solution.py:13
  86.9 9.3 %collective-permute-start.9 = (f32[2,1,16,320]{3,2,1,0:T(8,128)S(1)}, f32[2,1,16,320]{3,2,1,0:T(8,128)S(1)}, u32[]{:S(2)}, u32[]{:S(2)}) collective-permute-start(f32[2,1,16,320]{3,2,1,0:T(8,128)S(1)} %slice.1236), channel_id=1, source_target_pairs={{0,16},{16,32},{32,48},{48,64},{64,80},{80,96},{96,112},{1,17},{17... | collective-permute-start | bytes 122888 | tf_op jit(solution)/shard_map/ppermute | solution.py:13
  96.6 53.8 %copy-start.22 = (f32[16,16,320]{2,1,0:T(8,128)}, f32[16,16,320]{2,1,0:T(8,128)S(1)}, u32[]{:S(2)}) copy-start(f32[16,16,320]{2,1,0:T(8,128)S(1)} %get-tuple-element.110) | copy-start | bytes 983044
  96.6 53.8 %copy-start.23 = (f32[16,16,320]{2,1,0:T(8,128)}, f32[16,16,320]{2,1,0:T(8,128)S(1)}, u32[]{:S(2)}) copy-start(f32[16,16,320]{2,1,0:T(8,128)S(1)} %get-tuple-element.111) | copy-start | bytes 983044
  96.6 53.8 %copy-start.24 = (f32[16,16,320]{2,1,0:T(8,128)}, f32[16,16,320]{2,1,0:T(8,128)S(1)}, u32[]{:S(2)}) copy-start(f32[16,16,320]{2,1,0:T(8,128)S(1)} %get-tuple-element.112) | copy-start | bytes 983044
  97.3 6.3 %collective-permute-start.10 = (f32[2,1,16,320]{3,2,1,0:T(8,128)S(1)}, f32[2,1,16,320]{3,2,1,0:T(8,128)S(1)}, u32[]{:S(2)}, u32[]{:S(2)}) collective-permute-start(f32[2,1,16,320]{3,2,1,0:T(8,128)S(1)} %slice.1249), channel_id=1, source_target_pairs={{16,0},{32,16},{48,32},{64,48},{80,64},{96,80},{112,96},{17,1},{33... | collective-permute-start | bytes 122888 | tf_op jit(solution)/shard_map/ppermute | solution.py:13
  104.6 9.3 %collective-permute-start.11 = (f32[2,1,16,320]{3,2,1,0:T(8,128)S(1)}, f32[2,1,16,320]{3,2,1,0:T(8,128)S(1)}, u32[]{:S(2)}, u32[]{:S(2)}) collective-permute-start(f32[2,1,16,320]{3,2,1,0:T(8,128)S(1)} %slice.1260), channel_id=1, source_target_pairs={{0,16},{16,32},{32,48},{48,64},{64,80},{80,96},{96,112},{1,17},{17... | collective-permute-start | bytes 122888 | tf_op jit(solution)/shard_map/ppermute | solution.py:13
  113.9 1.3 copy-start.25
  115.5 6.3 %collective-permute-start.12 = (f32[2,1,16,320]{3,2,1,0:T(8,128)S(1)}, f32[2,1,16,320]{3,2,1,0:T(8,128)S(1)}, u32[]{:S(2)}, u32[]{:S(2)}) collective-permute-start(f32[2,1,16,320]{3,2,1,0:T(8,128)S(1)} %slice.1273), channel_id=1, source_target_pairs={{16,0},{32,16},{48,32},{64,48},{80,64},{96,80},{112,96},{17,1},{33... | collective-permute-start | bytes 122888 | tf_op jit(solution)/shard_map/ppermute | solution.py:13
  121.8 1.3 copy-start.2
  123.4 9.3 %collective-permute-start.13 = (f32[2,1,16,320]{3,2,1,0:T(8,128)S(1)}, f32[2,1,16,320]{3,2,1,0:T(8,128)S(1)}, u32[]{:S(2)}, u32[]{:S(2)}) collective-permute-start(f32[2,1,16,320]{3,2,1,0:T(8,128)S(1)} %slice.1284), channel_id=1, source_target_pairs={{0,16},{16,32},{32,48},{48,64},{64,80},{80,96},{96,112},{1,17},{17... | collective-permute-start | bytes 122888 | tf_op jit(solution)/shard_map/ppermute | solution.py:13
  133.5 6.3 %collective-permute-start.14 = (f32[2,1,16,320]{3,2,1,0:T(8,128)S(1)}, f32[2,1,16,320]{3,2,1,0:T(8,128)S(1)}, u32[]{:S(2)}, u32[]{:S(2)}) collective-permute-start(f32[2,1,16,320]{3,2,1,0:T(8,128)S(1)} %slice.1297), channel_id=1, source_target_pairs={{16,0},{32,16},{48,32},{64,48},{80,64},{96,80},{112,96},{17,1},{33... | collective-permute-start | bytes 122888 | tf_op jit(solution)/shard_map/ppermute | solution.py:13
  140.5 9.3 %collective-permute-start.15 = (f32[2,1,16,320]{3,2,1,0:T(8,128)S(1)}, f32[2,1,16,320]{3,2,1,0:T(8,128)S(1)}, u32[]{:S(2)}, u32[]{:S(2)}) collective-permute-start(f32[2,1,16,320]{3,2,1,0:T(8,128)S(1)} %slice.1308), channel_id=1, source_target_pairs={{0,16},{16,32},{32,48},{48,64},{64,80},{80,96},{96,112},{1,17},{17... | collective-permute-start | bytes 122888 | tf_op jit(solution)/shard_map/ppermute | solution.py:13
  150.9 6.5 %collective-permute-start.16 = (f32[2,1,16,320]{3,2,1,0:T(8,128)S(1)}, f32[2,1,16,320]{3,2,1,0:T(8,128)S(1)}, u32[]{:S(2)}, u32[]{:S(2)}) collective-permute-start(f32[2,1,16,320]{3,2,1,0:T(8,128)S(1)} %slice.1321), channel_id=1, source_target_pairs={{16,0},{32,16},{48,32},{64,48},{80,64},{96,80},{112,96},{17,1},{33... | collective-permute-start | bytes 122888 | tf_op jit(solution)/shard_map/ppermute | solution.py:13
  158.1 9.7 %collective-permute-start.17 = (f32[2,1,16,320]{3,2,1,0:T(8,128)S(1)}, f32[2,1,16,320]{3,2,1,0:T(8,128)S(1)}, u32[]{:S(2)}, u32[]{:S(2)}) collective-permute-start(f32[2,1,16,320]{3,2,1,0:T(8,128)S(1)} %slice.1332), channel_id=1, source_target_pairs={{0,16},{16,32},{32,48},{48,64},{64,80},{80,96},{96,112},{1,17},{17... | collective-permute-start | bytes 122888 | tf_op jit(solution)/shard_map/ppermute | solution.py:13
  168.7 6.3 %collective-permute-start.18 = (f32[2,1,16,320]{3,2,1,0:T(8,128)S(1)}, f32[2,1,16,320]{3,2,1,0:T(8,128)S(1)}, u32[]{:S(2)}, u32[]{:S(2)}) collective-permute-start(f32[2,1,16,320]{3,2,1,0:T(8,128)S(1)} %slice.1345), channel_id=1, source_target_pairs={{16,0},{32,16},{48,32},{64,48},{80,64},{96,80},{112,96},{17,1},{33... | collective-permute-start | bytes 122888 | tf_op jit(solution)/shard_map/ppermute | solution.py:13
  175.8 9.3 %collective-permute-start.19 = (f32[2,1,16,320]{3,2,1,0:T(8,128)S(1)}, f32[2,1,16,320]{3,2,1,0:T(8,128)S(1)}, u32[]{:S(2)}, u32[]{:S(2)}) collective-permute-start(f32[2,1,16,320]{3,2,1,0:T(8,128)S(1)} %slice.1356), channel_id=1, source_target_pairs={{0,16},{16,32},{32,48},{48,64},{64,80},{80,96},{96,112},{1,17},{17... | collective-permute-start | bytes 122888 | tf_op jit(solution)/shard_map/ppermute | solution.py:13
  185.9 6.3 %collective-permute-start.20 = (f32[2,1,16,320]{3,2,1,0:T(8,128)S(1)}, f32[2,1,16,320]{3,2,1,0:T(8,128)S(1)}, u32[]{:S(2)}, u32[]{:S(2)}) collective-permute-start(f32[2,1,16,320]{3,2,1,0:T(8,128)S(1)} %slice.1369), channel_id=1, source_target_pairs={{16,0},{32,16},{48,32},{64,48},{80,64},{96,80},{112,96},{17,1},{33... | collective-permute-start | bytes 122888 | tf_op jit(solution)/shard_map/ppermute | solution.py:13
  193.1 9.3 %collective-permute-start.21 = (f32[2,1,16,320]{3,2,1,0:T(8,128)S(1)}, f32[2,1,16,320]{3,2,1,0:T(8,128)S(1)}, u32[]{:S(2)}, u32[]{:S(2)}) collective-permute-start(f32[2,1,16,320]{3,2,1,0:T(8,128)S(1)} %slice.1380), channel_id=1, source_target_pairs={{0,16},{16,32},{32,48},{48,64},{64,80},{80,96},{96,112},{1,17},{17... | collective-permute-start | bytes 122888 | tf_op jit(solution)/shard_map/ppermute | solution.py:13
  203.5 1.2 copy-start.6
  203.6 1.4 copy-start.8
  (5 other events, 5.0 us)
Sparse Core Ops, SparseCore 0:
  204.6 68.8 reduce-scatter.1
